TPU v7x, 32 devices: a whole 2x2x4 slice. The times are simulated.
32 devices in a mesh: gz: 2 (over core), row: 4 (over y, x), col: 4 (over z).
Axes of the slice: x: 2, y: 2, z: 4, core: 2. Of those that a mesh axis runs over, the one named last changes fastest.
Arguments:
- l_panel: float32 [2, 8, 4, 8, 128, 256], P('gz', None, 'row', 'col'), may hold values from -6 to 6
- l_rows: int32 [2, 8, 4, 8], P('gz', None, 'row'), may hold values from -1 to 7, as said below
- u_panel: float32 [2, 8, 4, 16, 256, 128], P('gz', None, 'col', 'row'), may hold values from -0.125 to 0.125
- u_cols: int32 [2, 8, 4, 16], P('gz', None, 'col'), may hold values from -1 to 15, as said below
- u11_inv: float32 [2, 8, 256, 256], P('gz'), as said below
- ancestor: float32 [4, 1024, 8192], P('row', 'gz', 'col'), may hold values from -6 to 6
Outputs:
- schur: float32 [4, 1024, 8192], P('row', 'gz', 'col')
Inputs may be any that keep to these rules, and one draw needn't show every extreme that they name: `l_rows`: within one layer, supernode and process row the live entries are distinct; at most 8 are live, and in every layer and process row some supernode has all 8 live. `u_cols`: within one layer, supernode and process column the live entries are distinct; at most 16 are live, and in every layer and process column some supernode has all 16 live. `u11_inv`: upper triangular, with diagonal entries between 0.5 and 1.5.
All inputs are finite; a program needn't handle non-finite values.
Results may differ from a plain program's by a relative error of at most 0.000058.
Values sent between devices are 32-bit elements; how exact they have to be, the bound alone decides.
No kernel may reach another device: no remote copies, remote signals or barrier semaphores. Data moves between devices by JAX's collectives and lax.ppermute only.
A program may use at most 128 MiB of HBM per device.

v0:
```python
import jax
import jax.numpy as jnp
from jax import lax
from jax.sharding import PartitionSpec as P

W = 256
B = 128
AR = 8
AC = 16
highest = lax.Precision.HIGHEST


def place_rows(targets, blocks):
    onehot = (targets[:, None, :] == jnp.arange(AR, dtype=jnp.int32)[None, :, None]).astype(
        jnp.float32
    )
    return jnp.einsum("sak,skbw->absw", onehot, blocks, precision=highest)


def place_columns(targets, blocks):
    onehot = (targets[:, None, :] == jnp.arange(AC, dtype=jnp.int32)[None, :, None]).astype(
        jnp.float32
    )
    return jnp.einsum("sak,skwb->swab", onehot, blocks, precision=highest)


def body(l_panel, l_rows, u_panel, u_cols, u11_inv, ancestor):
    l_blocks = l_panel[0, :, 0]
    scaled = jnp.einsum("skbw,swv->skbv", l_blocks, u11_inv[0], precision=highest)
    row_targets = l_rows[0, :, 0]
    col_targets = u_cols[0, :, 0]
    u_blocks = u_panel[0, :, 0]
    supernodes = scaled.shape[0]
    targets = row_targets
    l_placed = place_rows(targets, lax.all_gather(scaled, "col", axis=1, tiled=True))
    targets = col_targets
    u_placed = place_columns(targets, lax.all_gather(u_blocks, "row", axis=1, tiled=True))
    l_matrix = l_placed.reshape(AR * B, supernodes * W)
    u_matrix = u_placed.reshape(supernodes * W, AC * B)
    half_rows = ancestor.shape[1]
    summed = lax.psum(jnp.dot(l_matrix, u_matrix, precision=highest), "gz")
    own_share = lax.dynamic_slice_in_dim(summed, lax.axis_index("gz") * half_rows, half_rows, 0)
    return ancestor - own_share[None]


def solution(mesh):
    in_specs = (
        P("gz", None, "row", "col", None, None),
        P("gz", None, "row", None),
        P("gz", None, "col", "row", None, None),
        P("gz", None, "col", None),
        P("gz", None, None, None),
        P("row", "gz", "col"),
    )
    out_specs = P("row", "gz", "col")
    return jax.shard_map(body, mesh=mesh, in_specs=in_specs, out_specs=out_specs, check_vma=False)
```

profile of v0, /device:TPU:0, one launch (start us, length us, event | category | flops | bytes accessed | tf_op | source)
XLA Modules:
  0.0 466.4 jit_solution(12975585213557576710)
XLA Ops:
  6.5 0.0 copy-start
  6.5 0.0 all-gather.4.cloned.1.call-start
  6.5 1.6 copy-done
  8.1 5.1 %fusion.11 = f32[8,2,128,256]{3,2,0,1:T(8,128)} fusion(f32[1,8,256,256]{3,2,1,0:T(8,128)S(1)} %copy-done, f32[1,8,1,2,128,256]{5,4,3,2,1,0:T(8,128)} %param.6), kind=kOutput, calls=%fused_computation.10 | convolution fusion | flops 1610612736 | bytes 6291456 | tf_op jit(solution)/shard_map/skbw,swv->skbv/dot_general | solution.py:29
  13.2 0.0 copy-start.4
  13.2 0.0 all-gather.4.cloned.1.call-update
  13.2 0.0 all-gather.6.cloned.1.call-start
  13.3 4.7 copy.13
  17.9 0.0 all-gather.6.cloned.1.call-update
  17.9 0.0 all-reduce.2.cloned.1.call-start
  18.0 147.7 %all-gather.4.cloned.1.call-done = f32[8,8,128,256]{3,2,0,1:T(8,128)} async-done(((f32[8,2,128,256]{3,2,0,1:T(8,128)}), f32[8,8,128,256]{3,2,0,1:T(8,128)}) %all-gather.4.cloned.1.call-update) | async-done | bytes 8388624 | tf_op jit(solution)/shard_map/all_gather | solution.py:35
  165.7 0.0 copy-done.4
  165.7 12.5 %fusion.8 = f32[8,128,8,256]{3,0,1,2:T(8,128)S(1)} fusion(f32[8,8,128,256]{3,2,0,1:T(8,128)} %all-gather.4.cloned.1.call-done, s32[8,8]{1,0:T(8,128)S(1)} %bitcast.41), kind=kOutput, calls=%fused_computation.9 | convolution fusion | flops 201327104 | bytes 16777472 | tf_op jit(solution)/shard_map/sak,skbw->absw/dot_general | solution.py:17
  178.2 4.9 %copy.12 = f32[8,128,8,256]{3,2,1,0:T(8,128)S(1)} copy(f32[8,128,8,256]{3,0,1,2:T(8,128)S(1)} %fusion.8) | data formatting | bytes 16777216 | tf_op jit(solution)/shard_map/sak,skbw->absw/transpose | solution.py:17
  183.0 0.0 copy-start.3
  183.0 7.3 %copy.19 = f32[128,8,8,256]{3,1,2,0:T(8,128)} copy(f32[128,8,8,256]{3,2,1,0:T(8,128)S(1)} %bitcast.38) | data formatting | bytes 16777216
  190.4 132.9 %all-gather.6.cloned.1.call-done = f32[1,8,1,16,256,128]{5,4,2,1,0,3:T(8,128)} async-done(((f32[1,8,1,4,256,128]{5,4,2,1,0,3:T(8,128)}), f32[1,8,1,16,256,128]{5,4,2,1,0,3:T(8,128)}) %all-gather.6.cloned.1.call-update) | async-done | bytes 16777232 | tf_op jit(solution)/shard_map/all_gather | solution.py:37
  323.2 0.0 copy-done.3
  323.2 0.0 copy-start.2
  323.2 25.9 %fusion.3 = f32[8,16,256,128]{3,1,2,0:T(8,128)} fusion(f32[1,8,1,16,256,128]{5,4,2,1,0,3:T(8,128)} %all-gather.6.cloned.1.call-done, s32[8,16]{1,0:T(8,128)S(1)} %bitcast.40), kind=kOutput, calls=%fused_computation.3 | convolution fusion | flops 805308416 | bytes 33554944 | tf_op jit(solution)/shard_map/sak,skwb->swab/dot_general | solution.py:24
  349.1 0.0 copy-done.2
  349.1 64.9 %fusion = f32[1024,2048]{1,0:T(8,128)} fusion(f32[1024,2048]{1,0:T(8,128)S(1)} %bitcast.39, f32[256,8,16,128]{3,2,1,0:T(8,128)} %bitcast.37), kind=kOutput, calls=%fused_computation | convolution fusion | flops 51539607552 | bytes 33554432 | tf_op jit(solution)/shard_map/dot_general | solution.py:41
  414.0 0.0 all-reduce.2.cloned.1.call-update
  414.0 0.0 copy-start.1
  414.0 39.0 %all-reduce.2.cloned.1.call-done = f32[1024,2048]{1,0:T(8,128)} async-done(((f32[1024,2048]{1,0:T(8,128)}), f32[1024,2048]{1,0:T(8,128)}) %all-reduce.2.cloned.1.call-update) | async-done | bytes 8388624 | tf_op jit(solution)/shard_map/psum | solution.py:41
  453.1 6.6 %bitcast_subtract_fusion = f32[1,512,2048]{2,1,0:T(8,128)} fusion(f32[1,512,2048]{2,1,0:T(8,128)} %param.11, f32[1024,2048]{1,0:T(8,128)} %all-reduce.2.cloned.1.call-done, s32[]{:T(128)S(6)} %select_n.3), kind=kLoop, calls=%fused_computation.8 | loop fusion | flops 1048576 | bytes 12582916 | tf_op jit(solution)/shard_map/sub | solution.py:43
  459.6 0.0 copy-done.1
Async XLA Ops:
  6.5 1.6 copy-start
  6.5 159.2 %all-gather.4.cloned.1.call-start = ((), (), s32[]{:S(2)}) async-start(), calls=%async_computation | async-start | bytes 10485760 | tf_op jit(solution)/shard_map/all_gather | solution.py:35
  13.2 152.5 %copy-start.4 = (s32[1,8,1,8]{3,2,1,0:T(1,128)S(1)}, s32[1,8,1,8]{3,2,1,0:T(1,128)}, u32[]{:S(2)}) copy-start(s32[1,8,1,8]{3,2,1,0:T(1,128)} %param.7) | copy-start | bytes 772
  13.2 310.0 %all-gather.6.cloned.1.call-start = ((), (), s32[]{:S(2)}) async-start(), calls=%async_computation.2 | async-start | bytes 20971520 | tf_op jit(solution)/shard_map/all_gather | solution.py:37
  17.9 435.1 %all-reduce.2.cloned.1.call-start = ((), (), s32[]{:S(2)}) async-start(), calls=%async_computation.1 | async-start | bytes 16777216 | tf_op jit(solution)/shard_map/psum | solution.py:41
  183.0 140.2 %copy-start.3 = (s32[1,8,1,16]{3,2,1,0:T(1,128)S(1)}, s32[1,8,1,16]{3,2,1,0:T(1,128)}, u32[]{:S(2)}) copy-start(s32[1,8,1,16]{3,2,1,0:T(1,128)} %param.9) | copy-start | bytes 1540
  323.2 25.9 %copy-start.2 = (f32[128,8,8,256]{3,1,2,0:T(8,128)S(1)}, f32[128,8,8,256]{3,1,2,0:T(8,128)}, u32[]{:S(2)}) copy-start(f32[128,8,8,256]{3,1,2,0:T(8,128)} %copy.19) | copy-start | bytes 25165828
  414.0 45.6 %copy-start.1 = (f32[1,8,256,256]{3,2,1,0:T(8,128)S(1)}, f32[1,8,256,256]{3,2,1,0:T(8,128)}, u32[]{:S(2)}) copy-start(f32[1,8,256,256]{3,2,1,0:T(8,128)} %param.10) | copy-start | bytes 6291460
Sparse Core Ops, SparseCore 0:
  13.3 152.3 all-gather.3
  167.5 155.6 all-gather.5
  414.2 38.8 all-reduce.1
where the time goes:
time: 472 us; the launch traced here: 466 us
  waiting for transfers between devices  320 us (68%)
  matrix products  108 us (23%)
  local copies, waits for them, and re-layouts  18.4 us (4%)
  between operations  13.4 us (3%)
  other arithmetic  6.56 us (1%)
    all_gather x1, waiting for transfers between devices, body(): lax.all_gather(scaled, 'col', axis=1, tiled=True)  148 us
    all_gather x1, waiting for transfers between devices, body(): lax.all_gather(u_blocks, 'row', axis=1, tiled=True)  133 us
    dot_general x1, matrix products, body(): summed = lax.psum(jnp.dot(l_matrix, u_matrix, precision=highest), 'gz')  64.9 us
    psum x1, waiting for transfers between devices, body(): summed = lax.psum(jnp.dot(l_matrix, u_matrix, precision=highest), 'gz')  39 us
    dot_general x1, matrix products, place_columns(): return jnp.einsum('sak,skwb->swab', onehot, blocks, precision=highest)  25.9 us
    unnamed x12, local copies, waits for them, and re-layouts  13.6 us
    dot_general x1, matrix products, place_rows(): return jnp.einsum('sak,skbw->absw', onehot, blocks, precision=highest)  12.5 us
  transfers between devices with their start and end apart: 3, of which 3 were waited for; matrix products, arithmetic and copies ran while one was open for 6% of the time, Pallas kernels for 0%

commit v1 on v0

--- a/solution.py
+++ b/solution.py
@@ -8,6 +8,19 @@
 AR = 8
 AC = 16
 highest = lax.Precision.HIGHEST
+
+
+def gather_around(x, axis, dim):
+    ways = lax.axis_size(axis)
+    up = [(d, (d + 1) % ways) for d in range(ways)]
+    down = [(d, (d - 1) % ways) for d in range(ways)]
+    earlier, later = ([x], [x])
+    for _ in range(ways // 2):
+        earlier.append(lax.ppermute(earlier[-1], axis, up))
+    for _ in range((ways - 1) // 2):
+        later.append(lax.ppermute(later[-1], axis, down))
+    line = jnp.concatenate([*earlier[::-1], *later[1:]], axis=dim)
+    return jnp.roll(line, (lax.axis_index(axis) - ways // 2) * x.shape[dim], axis=dim)
 
 
 def place_rows(targets, blocks):
@@ -34,7 +47,7 @@
     targets = row_targets
     l_placed = place_rows(targets, lax.all_gather(scaled, "col", axis=1, tiled=True))
     targets = col_targets
-    u_placed = place_columns(targets, lax.all_gather(u_blocks, "row", axis=1, tiled=True))
+    u_placed = place_columns(targets, gather_around(u_blocks, "row", 1))
     l_matrix = l_placed.reshape(AR * B, supernodes * W)
     u_matrix = u_placed.reshape(supernodes * W, AC * B)
     half_rows = ancestor.shape[1]

time: 472 us -> 542 us (1.15)
  local copies, waits for them, and re-layouts: 18.4 us -> 99.7 us
  waiting for transfers between devices: 320 us -> 309 us
  matrix products: 108 us -> 101 us
    ppermute x0 -> x3, waiting for transfers between devices: none -> 269 us  [the longest x2 180 us: gather_around(): earlier.append(lax.ppermute(earlier[-1], axis, up))]
    all_gather x1, waiting for transfers between devices: 148 us -> 0.01 us  [body(): lax.all_gather(scaled, 'col', axis=1, tiled=True)]
    all_gather x1 -> x0, waiting for transfers between devices: 133 us -> none  [body(): lax.all_gather(u_blocks, 'row', axis=1, tiled=True)]
    concatenate x0 -> x1, local copies, waits for them, and re-layouts: none -> 82.2 us  [gather_around(): jnp.roll(line, (lax.axis_index(axis) - ways // 2) * x.shape[dim], axis=dim)]
    dot_general x1, matrix products: 25.9 us -> 17.1 us  [place_columns(): return jnp.einsum('sak,skwb->swab', onehot, blocks, precision=highest)]
    ppermute x0 -> x3, starting transfers between devices: none -> 5.45 us  [the longest x2 4.49 us: gather_around(): earlier.append(lax.ppermute(earlier[-1], axis, up))]
    unnamed x12 -> x10, local copies, waits for them, and re-layouts: 13.6 us -> 12.6 us
  transfers between devices with their start and end apart: 3 -> 5, of which waited for: 3 -> 4; matrix products, arithmetic and copies ran while one was open for 6% -> 20% of each run, Pallas kernels for 0% -> 0%
where the time goes in v1:
time: 542 us; the launch traced here: 535 us
  waiting for transfers between devices  309 us (57%)
  matrix products  101 us (19%)
  local copies, waits for them, and re-layouts  99.7 us (18%)
  between operations  13.7 us (3%)
  other arithmetic  6.56 us (1%)
  starting transfers between devices  5.49 us (1%)
    ppermute x2, waiting for transfers between devices, gather_around(): earlier.append(lax.ppermute(earlier[-1], axis, up))  180 us
    ppermute x1, waiting for transfers between devices, gather_around(): later.append(lax.ppermute(later[-1], axis, down))  88.9 us
    concatenate x1, local copies, waits for them, and re-layouts, gather_around(): jnp.roll(line, (lax.axis_index(axis) - ways // 2) * x.shape[dim], axis=dim)  82.2 us
    dot_general x1, matrix products, body(): summed = lax.psum(jnp.dot(l_matrix, u_matrix, precision=highest), 'gz')  67.1 us
    psum x1, waiting for transfers between devices, body(): summed = lax.psum(jnp.dot(l_matrix, u_matrix, precision=highest), 'gz')  39.6 us
    dot_general x1, matrix products, place_columns(): return jnp.einsum('sak,skwb->swab', onehot, blocks, precision=highest)  17.1 us
    unnamed x10, local copies, waits for them, and re-layouts  12.6 us
    dot_general x1, matrix products, place_rows(): return jnp.einsum('sak,skbw->absw', onehot, blocks, precision=highest)  12.2 us
  transfers between devices with their start and end apart: 5, of which 4 were waited for; matrix products, arithmetic and copies ran while one was open for 20% of the time, Pallas kernels for 0%

profile of v1, /device:TPU:0, one launch (start us, length us, event | category | flops | bytes accessed | tf_op | source)
XLA Modules:
  0.0 535.4 jit_solution(1573533660231461790)
XLA Ops:
  6.5 0.0 copy-start
  6.5 0.0 all-gather.2.cloned.1.call-start
  6.5 1.6 copy-done
  8.1 5.0 fusion.10
  13.2 0.0 all-gather.2.cloned.1.call-update
  13.2 0.0 all-reduce.2.cloned.1.call-start
  13.2 6.9 %copy.31 = f32[1,8,1,4,256,128]{5,3,4,1,2,0:T(4,128)} copy(f32[1,8,1,4,256,128]{5,4,3,2,1,0:T(8,128)} %param.8) | data formatting | bytes 8388608 | tf_op args[2]
  20.1 2.9 collective-permute-start
  23.1 1.0 collective-permute-start.2
  24.0 91.7 %collective-permute-done = f32[8,4,256,128]{3,1,2,0:T(4,128)} collective-permute-done((f32[8,4,256,128]{3,1,2,0:T(4,128)}, f32[8,4,256,128]{3,1,2,0:T(4,128)}, u32[]{:S(2)}, u32[]{:S(2)}) %collective-permute-start) | collective-permute-done | bytes 4194336 | tf_op jit(solution)/shard_map/ppermute | solution.py:19
  115.8 1.5 collective-permute-start.1
  117.3 0.0 copy-start.2
  117.3 88.9 %collective-permute-done.2 = f32[8,4,256,128]{3,1,2,0:T(4,128)} collective-permute-done((f32[8,4,256,128]{3,1,2,0:T(4,128)}, f32[8,4,256,128]{3,1,2,0:T(4,128)}, u32[]{:S(2)}, u32[]{:S(2)}) %collective-permute-start.2) | collective-permute-done | bytes 4194336 | tf_op jit(solution)/shard_map/ppermute | solution.py:21
  206.2 88.5 %collective-permute-done.1 = f32[8,4,256,128]{3,1,2,0:T(4,128)} collective-permute-done((f32[8,4,256,128]{3,1,2,0:T(4,128)}, f32[8,4,256,128]{3,1,2,0:T(4,128)}, u32[]{:S(2)}, u32[]{:S(2)}) %collective-permute-start.1) | collective-permute-done | bytes 4194336 | tf_op jit(solution)/shard_map/ppermute | solution.py:19
  294.7 82.2 %concatenate.6 = f32[8,32,256,128]{3,1,2,0:T(8,128)} concatenate(f32[8,4,256,128]{3,1,2,0:T(4,128)} %collective-permute-done.1, f32[8,4,256,128]{3,1,2,0:T(4,128)} %collective-permute-done, f32[8,4,256,128]{3,1,2,0:T(4,128)} %bitcast.36, f32[8,4,256,128]{3,1,2,0:T(4,128)} %collective-permute-done.2, f32[8,4,256,128]{3,1,2,0:T(4,128)} %collective-permute-done.1, ...), dimensions={1} | concatenate | bytes 67108864 | tf_op jit(solution)/shard_map/jit(_roll_dynamic)/concatenate | solution.py:23
  376.9 0.0 copy-done.2
  376.9 0.0 copy-start.3
  376.9 17.1 %fusion.3 = f32[8,256,128,16]{2,3,1,0:T(8,128)} fusion(f32[8,32,256,128]{3,1,2,0:T(8,128)} %concatenate.6, s32[]{:T(128)S(6)} %select_n.17, s32[8,16]{1,0:T(8,128)S(1)} %bitcast.40), kind=kOutput, calls=%fused_computation.3 | convolution fusion | flops 805308416 | bytes 33554948 | tf_op jit(solution)/shard_map/sak,skwb->swab/dot_general | solution.py:37
  393.9 0.0 all-gather.2.cloned.1.call-done
  394.0 0.0 copy-done.3
  394.0 12.2 %fusion.7 = f32[8,128,8,256]{3,0,1,2:T(8,128)S(1)} fusion(f32[8,8,128,256]{3,2,0,1:T(8,128)} %all-gather.2.cloned.1.call-done, s32[8,8]{1,0:T(8,128)S(1)} %bitcast.41), kind=kOutput, calls=%fused_computation.9 | convolution fusion | flops 201327104 | bytes 16777472 | tf_op jit(solution)/shard_map/sak,skbw->absw/dot_general | solution.py:30
  406.1 4.9 copy.12
  411.0 4.1 copy.18
  415.1 67.1 %fusion = f32[1024,2048]{1,0:T(8,128)} fusion(f32[1024,2048]{1,0:T(8,128)S(1)} %bitcast.39, f32[256,8,16,128]{3,2,1,0:T(8,128)} %bitcast.37), kind=kOutput, calls=%fused_computation | convolution fusion | flops 51539607552 | bytes 33554432 | tf_op jit(solution)/shard_map/dot_general | solution.py:54
  482.2 0.0 all-reduce.2.cloned.1.call-update
  482.2 0.0 copy-start.1
  482.2 39.6 %all-reduce.2.cloned.1.call-done = f32[1024,2048]{1,0:T(8,128)} async-done(((f32[1024,2048]{1,0:T(8,128)}), f32[1024,2048]{1,0:T(8,128)}) %all-reduce.2.cloned.1.call-update) | async-done | bytes 8388624 | tf_op jit(solution)/shard_map/psum | solution.py:54
  521.8 6.6 %bitcast_subtract_fusion = f32[1,512,2048]{2,1,0:T(8,128)} fusion(f32[1,512,2048]{2,1,0:T(8,128)} %param.11, f32[1024,2048]{1,0:T(8,128)} %all-reduce.2.cloned.1.call-done, s32[]{:T(128)S(6)} %select_n.18), kind=kLoop, calls=%fused_computation.7 | loop fusion | flops 1048576 | bytes 12582916 | tf_op jit(solution)/shard_map/sub | solution.py:56
  528.3 0.0 copy-done.1
Async XLA Ops:
  6.5 1.6 copy-start
  6.5 387.4 %all-gather.2.cloned.1.call-start = ((), (), s32[]{:S(2)}) async-start(), calls=%async_computation | async-start | bytes 10485760 | tf_op jit(solution)/shard_map/all_gather | solution.py:48
  13.2 508.6 %all-reduce.2.cloned.1.call-start = ((), (), s32[]{:S(2)}) async-start(), calls=%async_computation.1 | async-start | bytes 16777216 | tf_op jit(solution)/shard_map/psum | solution.py:54
  20.1 95.6 %collective-permute-start = (f32[8,4,256,128]{3,1,2,0:T(4,128)}, f32[8,4,256,128]{3,1,2,0:T(4,128)}, u32[]{:S(2)}, u32[]{:S(2)}) collective-permute-start(f32[8,4,256,128]{3,1,2,0:T(4,128)} %bitcast.36), channel_id=1, source_target_pairs={{0,4},{4,8},{8,12},{12,0},{1,5},{5,9},{9,13},{13,1},{2,6},{6,10},{... | collective-permute-start | bytes 12582920 | tf_op jit(solution)/shard_map/ppermute | solution.py:19
  23.1 183.1 %collective-permute-start.2 = (f32[8,4,256,128]{3,1,2,0:T(4,128)}, f32[8,4,256,128]{3,1,2,0:T(4,128)}, u32[]{:S(2)}, u32[]{:S(2)}) collective-permute-start(f32[8,4,256,128]{3,1,2,0:T(4,128)} %bitcast.36), channel_id=1, source_target_pairs={{0,12},{4,0},{8,4},{12,8},{1,13},{5,1},{9,5},{13,9},{2,14},{6,2},{... | collective-permute-start | bytes 12582920 | tf_op jit(solution)/shard_map/ppermute | solution.py:21
  115.8 178.9 %collective-permute-start.1 = (f32[8,4,256,128]{3,1,2,0:T(4,128)}, f32[8,4,256,128]{3,1,2,0:T(4,128)}, u32[]{:S(2)}, u32[]{:S(2)}) collective-permute-start(f32[8,4,256,128]{3,1,2,0:T(4,128)} %collective-permute-done), channel_id=1, source_target_pairs={{0,4},{4,8},{8,12},{12,0},{1,5},{5,9},{9,13},{13,1},{2,6},{6,10},{... | collective-permute-start | bytes 12582920 | tf_op jit(solution)/shard_map/ppermute | solution.py:19
  117.3 259.6 %copy-start.2 = (s32[1,8,1,16]{3,2,1,0:T(1,128)S(1)}, s32[1,8,1,16]{3,2,1,0:T(1,128)}, u32[]{:S(2)}) copy-start(s32[1,8,1,16]{3,2,1,0:T(1,128)} %param.9) | copy-start | bytes 1540
  376.9 17.1 %copy-start.3 = (s32[1,8,1,8]{3,2,1,0:T(1,128)S(1)}, s32[1,8,1,8]{3,2,1,0:T(1,128)}, u32[]{:S(2)}) copy-start(s32[1,8,1,8]{3,2,1,0:T(1,128)} %param.7) | copy-start | bytes 772
  482.2 46.1 %copy-start.1 = (f32[1,8,256,256]{3,2,1,0:T(8,128)S(1)}, f32[1,8,256,256]{3,2,1,0:T(8,128)}, u32[]{:S(2)}) copy-start(f32[1,8,256,256]{3,2,1,0:T(8,128)} %param.10) | copy-start | bytes 6291460
Sparse Core Ops, SparseCore 0:
  13.3 152.3 all-gather.1
  482.3 39.4 all-reduce.1
